TPU v7x, 32 devices: a whole 2x2x4 slice. The times are simulated.
32 devices in a mesh: rows: 8 (over z, y), dims: 4 (over x, core).
Axes of the slice: x: 2, y: 2, z: 4, core: 2. Of those that a mesh axis runs over, the one named last changes fastest.
Arguments:
- table: bfloat16 [1, 256, 32768], P(None, 'dims', 'rows'), may hold values from -6 to 6
- accum: float32 [1, 32768], P(None, 'rows'), may hold values from 0.5 to 8
- grad_pooled: bfloat16 [1, 256, 1024], P(None, 'dims', 'rows'), may hold values from -6 to 6
- sample_slot: int32 [1, 8, 8, 1280], P(None, 'rows'), may hold values from 0 to 127
- row_slot: int32 [1, 8, 8, 1280], P(None, 'rows'), may hold values from 0 to 4095
- weight: int32 [1, 8, 8, 1280], P(None, 'rows'), may hold values from 1 to 3
- send_count: int32 [1, 8, 8], P(None, 'rows'), may hold values from 1 to 1280, as said below
Outputs:
- pooled: float32 [1, 256, 1024], P(None, 'dims', 'rows')
- new_table: bfloat16 [1, 256, 32768], P(None, 'dims', 'rows')
- new_accum: float32 [1, 32768], P(None, 'rows')
Inputs may be any that keep to these rules, and one draw needn't show every extreme that they name: `send_count`: at most 1280 live entries from one row shard to one owner per feature; in every feature one owner receives exactly 1280 from every row shard. Slots at or after the count are unused.
All inputs are finite; a program needn't handle non-finite values.
Results may differ from a plain program's by a relative error of at most 0.001.
Values may be sent and summed in bfloat16 or wider, within the bound.
No kernel may reach another device: no remote copies, remote signals or barrier semaphores. Data moves between devices by JAX's collectives and lax.ppermute only.
A program may use at most 64 MiB of HBM per device.

v0:
```python
import math
import jax
import jax.numpy as jnp
from jax import lax
from jax.sharding import PartitionSpec as P

D = 256
step_size = 0.3


def shards(table, accum, grad_pooled, sample_slot, row_slot, weight, send_count):
    feat_count, dim_local, row_local = table.shape
    peer_count = lax.axis_size("rows")
    own_samples = grad_pooled.shape[2]
    slot_count = sample_slot.shape[3]
    entry_count = peer_count * slot_count
    block_rows = math.gcd(row_local, 512)
    block_count = row_local // block_rows
    sample_local = sample_slot.reshape(feat_count, peer_count, slot_count)
    row_index = row_slot.reshape(feat_count, peer_count, slot_count)
    flat_rows = row_index.reshape(feat_count, 1, entry_count)
    live_count = send_count.reshape(feat_count, peer_count)
    slot_iota = lax.broadcasted_iota(jnp.int32, (1, 1, slot_count), 2)
    live_mask = slot_iota < live_count[:, :, None]
    weights = jnp.where(live_mask, weight.reshape(feat_count, peer_count, slot_count), 0)
    flat_weights = weights.reshape(feat_count, 1, entry_count).astype(jnp.bfloat16)
    block_iota = lax.broadcasted_iota(jnp.int32, (1, block_rows, 1), 1)

    def lookup_block(carry, block):
        start = block * block_rows
        table_part = lax.dynamic_slice_in_dim(table, start, block_rows, 2)
        selector = (flat_rows == block_iota + start).astype(jnp.bfloat16)
        return (
            carry
            + jnp.einsum("fdr,fre->fde", table_part, selector, preferred_element_type=jnp.float32),
            None,
        )

    looked_up, _ = lax.scan(
        lookup_block,
        jnp.zeros((feat_count, dim_local, entry_count), jnp.float32),
        jnp.arange(block_count, dtype=jnp.int32),
    )
    picked = looked_up.astype(jnp.bfloat16).reshape(feat_count, dim_local, peer_count, slot_count)
    positions = lax.broadcasted_iota(jnp.int32, (1, 1, 1, own_samples), 3)
    onehot = jnp.where(sample_local[..., None] == positions, weights[..., None], 0).astype(
        jnp.bfloat16
    )
    pooled = lax.psum_scatter(
        jnp.einsum("fdnk,fnkj->nfdj", picked, onehot, preferred_element_type=jnp.float32),
        "rows",
        scatter_dimension=0,
        tiled=True,
    ).reshape(feat_count, dim_local, own_samples)
    all_grads = lax.all_gather(grad_pooled, "rows", axis=2, tiled=True)
    all_grads = all_grads.reshape(feat_count, dim_local, peer_count, own_samples)
    selector = (sample_local[..., None] == positions).astype(jnp.bfloat16)
    entry_values = jnp.einsum(
        "fdnj,fnkj->fdnk", all_grads, selector, preferred_element_type=jnp.float32
    ).astype(jnp.bfloat16)
    entry_flat = entry_values.reshape(feat_count, dim_local, entry_count)

    def gradient_block(block):
        start = block * block_rows
        weighted = jnp.where(flat_rows == block_iota + start, flat_weights, 0)
        return jnp.einsum("fde,fre->fdr", entry_flat, weighted, preferred_element_type=jnp.float32)

    grad_blocks = lax.map(gradient_block, jnp.arange(block_count, dtype=jnp.int32))
    row_grad = jnp.moveaxis(grad_blocks, 0, 2).reshape(feat_count, dim_local, row_local)
    squares = jnp.sum(row_grad * row_grad, axis=1)
    norm_total = lax.psum(squares, "dims")
    new_accum = accum + norm_total / D
    new_table = (
        table.astype(jnp.float32) - step_size * row_grad / jnp.sqrt(new_accum)[:, None, :]
    ).astype(jnp.bfloat16)
    return (pooled, new_table, new_accum)


def solution(mesh):
    return jax.shard_map(
        shards,
        mesh=mesh,
        in_specs=(
            P(None, "dims", "rows"),
            P(None, "rows"),
            P(None, "dims", "rows"),
            P(None, "rows", None, None),
            P(None, "rows", None, None),
            P(None, "rows", None, None),
            P(None, "rows", None),
        ),
        out_specs=(P(None, "dims", "rows"), P(None, "dims", "rows"), P(None, "rows")),
        check_vma=False,
    )
```

profile of v0, /device:TPU:0, one launch (start us, length us, event | category | flops | bytes accessed | tf_op | source)
XLA Modules:
  0.0 151.7 jit_solution(12816893557992294160)
XLA Ops:
  7.2 0.0 reduce-scatter.2.cloned.1.call-start
  7.2 0.8 reshape_reshape.3
  8.1 48.6 %while.25 = (s32[]{:T(128)}, f32[1,64,10240]{2,1,0:T(8,128)S(1)}, s32[8]{0:T(128)S(1)}, bf16[1,64,4096]{2,1,0:T(8,128)(2,1)}, s32[1,1,10240]{2,1,0:T(1,128)S(1)}...) while((s32[]{:T(128)}, f32[1,64,10240]{2,1,0:T(8,128)S(1)}, s32[8]{0:T(128)S(1)}, ...), condition=%wide.region_1.2_spmd.clone, body=%wide.region_0.1_spmd.clone.sunk | while | flops 677642752 | bytes 5353649 | solution.py:39
  8.1 0.6 dynamic_slice.25
  9.3 4.8 %fusion.55 = f32[1,64,10240]{2,1,0:T(8,128)S(1)} fusion(s32[10240]{0:T(1024)S(1)} %bitcast.90, s32[512]{0:T(512)S(1)} %bitcast.88, f32[1,64,10240]{2,1,0:T(8,128)S(1)} %get-tuple-element.264, pred[]{:T(512)S(6)} %compare.3, bf16[1,64,4096]{2,1,0:T(8,128)(2,1)} %get-tuple-element.275, s32[]{:T(128)S(6)} %select_n.63), kind=kOutput, calls=%fused_computation.5.clone.1 | convolution fusion | flops 677642240 | bytes 5351429 | tf_op jit(solution)/shard_map/while/body/eval_jaxpr/fdr,fre->fde/dot_general | solution.py:35
  14.1 0.6 dynamic_slice.25
  15.4 4.8 %fusion.55 = f32[1,64,10240]{2,1,0:T(8,128)S(1)} fusion(s32[10240]{0:T(1024)S(1)} %bitcast.90, s32[512]{0:T(512)S(1)} %bitcast.88, f32[1,64,10240]{2,1,0:T(8,128)S(1)} %get-tuple-element.264, pred[]{:T(512)S(6)} %compare.3, bf16[1,64,4096]{2,1,0:T(8,128)(2,1)} %get-tuple-element.275, s32[]{:T(128)S(6)} %select_n.63), kind=kOutput, calls=%fused_computation.5.clone.1 | convolution fusion | flops 677642240 | bytes 5351429 | tf_op jit(solution)/shard_map/while/body/eval_jaxpr/fdr,fre->fde/dot_general | solution.py:35
  20.2 0.6 dynamic_slice.25
  21.5 4.8 %fusion.55 = f32[1,64,10240]{2,1,0:T(8,128)S(1)} fusion(s32[10240]{0:T(1024)S(1)} %bitcast.90, s32[512]{0:T(512)S(1)} %bitcast.88, f32[1,64,10240]{2,1,0:T(8,128)S(1)} %get-tuple-element.264, pred[]{:T(512)S(6)} %compare.3, bf16[1,64,4096]{2,1,0:T(8,128)(2,1)} %get-tuple-element.275, s32[]{:T(128)S(6)} %select_n.63), kind=kOutput, calls=%fused_computation.5.clone.1 | convolution fusion | flops 677642240 | bytes 5351429 | tf_op jit(solution)/shard_map/while/body/eval_jaxpr/fdr,fre->fde/dot_general | solution.py:35
  26.3 0.6 dynamic_slice.25
  27.5 4.8 %fusion.55 = f32[1,64,10240]{2,1,0:T(8,128)S(1)} fusion(s32[10240]{0:T(1024)S(1)} %bitcast.90, s32[512]{0:T(512)S(1)} %bitcast.88, f32[1,64,10240]{2,1,0:T(8,128)S(1)} %get-tuple-element.264, pred[]{:T(512)S(6)} %compare.3, bf16[1,64,4096]{2,1,0:T(8,128)(2,1)} %get-tuple-element.275, s32[]{:T(128)S(6)} %select_n.63), kind=kOutput, calls=%fused_computation.5.clone.1 | convolution fusion | flops 677642240 | bytes 5351429 | tf_op jit(solution)/shard_map/while/body/eval_jaxpr/fdr,fre->fde/dot_general | solution.py:35
  32.4 0.6 dynamic_slice.25
  33.6 4.8 %fusion.55 = f32[1,64,10240]{2,1,0:T(8,128)S(1)} fusion(s32[10240]{0:T(1024)S(1)} %bitcast.90, s32[512]{0:T(512)S(1)} %bitcast.88, f32[1,64,10240]{2,1,0:T(8,128)S(1)} %get-tuple-element.264, pred[]{:T(512)S(6)} %compare.3, bf16[1,64,4096]{2,1,0:T(8,128)(2,1)} %get-tuple-element.275, s32[]{:T(128)S(6)} %select_n.63), kind=kOutput, calls=%fused_computation.5.clone.1 | convolution fusion | flops 677642240 | bytes 5351429 | tf_op jit(solution)/shard_map/while/body/eval_jaxpr/fdr,fre->fde/dot_general | solution.py:35
  38.4 0.6 dynamic_slice.25
  39.7 4.8 %fusion.55 = f32[1,64,10240]{2,1,0:T(8,128)S(1)} fusion(s32[10240]{0:T(1024)S(1)} %bitcast.90, s32[512]{0:T(512)S(1)} %bitcast.88, f32[1,64,10240]{2,1,0:T(8,128)S(1)} %get-tuple-element.264, pred[]{:T(512)S(6)} %compare.3, bf16[1,64,4096]{2,1,0:T(8,128)(2,1)} %get-tuple-element.275, s32[]{:T(128)S(6)} %select_n.63), kind=kOutput, calls=%fused_computation.5.clone.1 | convolution fusion | flops 677642240 | bytes 5351429 | tf_op jit(solution)/shard_map/while/body/eval_jaxpr/fdr,fre->fde/dot_general | solution.py:35
  44.5 0.6 dynamic_slice.25
  45.8 4.8 %fusion.55 = f32[1,64,10240]{2,1,0:T(8,128)S(1)} fusion(s32[10240]{0:T(1024)S(1)} %bitcast.90, s32[512]{0:T(512)S(1)} %bitcast.88, f32[1,64,10240]{2,1,0:T(8,128)S(1)} %get-tuple-element.264, pred[]{:T(512)S(6)} %compare.3, bf16[1,64,4096]{2,1,0:T(8,128)(2,1)} %get-tuple-element.275, s32[]{:T(128)S(6)} %select_n.63), kind=kOutput, calls=%fused_computation.5.clone.1 | convolution fusion | flops 677642240 | bytes 5351429 | tf_op jit(solution)/shard_map/while/body/eval_jaxpr/fdr,fre->fde/dot_general | solution.py:35
  50.6 0.6 dynamic_slice.25
  51.8 4.8 %fusion.55 = f32[1,64,10240]{2,1,0:T(8,128)S(1)} fusion(s32[10240]{0:T(1024)S(1)} %bitcast.90, s32[512]{0:T(512)S(1)} %bitcast.88, f32[1,64,10240]{2,1,0:T(8,128)S(1)} %get-tuple-element.264, pred[]{:T(512)S(6)} %compare.3, bf16[1,64,4096]{2,1,0:T(8,128)(2,1)} %get-tuple-element.275, s32[]{:T(128)S(6)} %select_n.63), kind=kOutput, calls=%fused_computation.5.clone.1 | convolution fusion | flops 677642240 | bytes 5351429 | tf_op jit(solution)/shard_map/while/body/eval_jaxpr/fdr,fre->fde/dot_general | solution.py:35
  56.6 0.0 copy-start.1
  56.6 0.0 copy-start.4
  56.7 0.0 copy-start.5
  56.7 0.1 convert_element_type.41
  56.8 0.2 copy.18
  57.0 0.4 copy-done.1
  57.4 0.1 bitcast_select_fusion
  57.5 5.2 %fusion.39 = f32[8,1,64,128]{3,2,0,1:T(8,128)} fusion(s32[8,1280]{1,0:T(8,128)S(1)} %bitcast_select_fusion, s32[8,1280]{1,0:T(8,128)S(1)} %bitcast.94, bf16[64,8,1280]{2,1,0:T(8,128)(2,1)S(1)} %bitcast.82), kind=kOutput, calls=%fused_computation.34 | convolution fusion | flops 171704320 | bytes 1654784 | tf_op jit(solution)/shard_map/fdnk,fnkj->nfdj/dot_general | solution.py:50
  62.6 0.0 reduce-scatter.2.cloned.1.call-update
  62.8 0.1 lt.56
  62.9 28.1 %all_gather.3 = bf16[1,64,1024]{2,1,0:T(8,128)(2,1)S(1)} all-gather(bf16[1,64,128]{2,1,0:T(8,128)(2,1)S(1)} %copy-done.2), channel_id=1, replica_groups=mesh['rows'=8,'dims'=4] {'rows'}, dimensions={2}, use_global_device_ids=true | all-gather | bytes 147456 | tf_op jit(solution)/shard_map/all_gather | solution.py:55
  91.0 3.1 %fusion.32 = bf16[1,8,8,8,1280]{4,3,2,1,0:T(8,128)(2,1)S(1)} fusion(s32[8,1280]{1,0:T(8,128)S(1)} %bitcast.95, bf16[64,8,128]{2,1,0:T(8,128)(2,1)S(1)} %bitcast.84), kind=kOutput, calls=%fused_computation.27 | convolution fusion | flops 169738240 | bytes 1482752 | tf_op jit(solution)/shard_map/fdnj,fnkj->fdnk/dot_general | solution.py:58
  94.2 0.1 copy.16
  94.3 0.1 fusion.43
  94.3 38.5 %while.24 = (s32[]{:T(128)}, f32[8,1,64,512]{3,2,1,0:T(8,128)S(1)}, s32[1,1,10240]{2,1,0:T(1,128)S(1)}, s32[8]{0:T(128)S(1)}, bf16[1,1,10240]{2,1,0:T(2,128)(2,1...) while((s32[]{:T(128)}, f32[8,1,64,512]{3,2,1,0:T(8,128)S(1)}, ...), condition=%wide.region_4.5_spmd.clone, body=%wide.region_3.4_spmd.clone.sunk | while | flops 681574912 | bytes 1548423 | solution.py:68
  94.4 0.6 dynamic_slice.23
  95.6 0.1 reduce.5
  95.7 3.4 %fusion.52 = f32[8,1,64,512]{3,2,1,0:T(8,128)S(1)} fusion(f32[8,1,64,512]{3,2,1,0:T(8,128)S(1)} %get-tuple-element.291, s32[]{:T(128)S(6)} %copy.36, bf16[1,64,10240]{2,1,0:T(8,128)(2,1)S(1)} %get-tuple-element.304, s32[10240]{0:T(1024)S(1)} %bitcast.91, s32[512]{0:T(512)S(1)} %bitcast.89, bf16[10240]{0:T(1024)(128)(2,1)S(1)} %reduce.5), kind=kOutput, calls=%fused_computation.20.clone.1 | convolution fusion | flops 681574400 | bytes 1505284 | tf_op jit(solution)/shard_map/while/body/eval_jaxpr/fde,fre->fdr/dot_general | solution.py:66
  99.2 0.6 dynamic_slice.23
  100.4 0.1 reduce.5
  100.5 3.4 %fusion.52 = f32[8,1,64,512]{3,2,1,0:T(8,128)S(1)} fusion(f32[8,1,64,512]{3,2,1,0:T(8,128)S(1)} %get-tuple-element.291, s32[]{:T(128)S(6)} %copy.36, bf16[1,64,10240]{2,1,0:T(8,128)(2,1)S(1)} %get-tuple-element.304, s32[10240]{0:T(1024)S(1)} %bitcast.91, s32[512]{0:T(512)S(1)} %bitcast.89, bf16[10240]{0:T(1024)(128)(2,1)S(1)} %reduce.5), kind=kOutput, calls=%fused_computation.20.clone.1 | convolution fusion | flops 681574400 | bytes 1505284 | tf_op jit(solution)/shard_map/while/body/eval_jaxpr/fde,fre->fdr/dot_general | solution.py:66
  104.0 0.6 dynamic_slice.23
  105.2 0.1 reduce.5
  105.3 3.4 %fusion.52 = f32[8,1,64,512]{3,2,1,0:T(8,128)S(1)} fusion(f32[8,1,64,512]{3,2,1,0:T(8,128)S(1)} %get-tuple-element.291, s32[]{:T(128)S(6)} %copy.36, bf16[1,64,10240]{2,1,0:T(8,128)(2,1)S(1)} %get-tuple-element.304, s32[10240]{0:T(1024)S(1)} %bitcast.91, s32[512]{0:T(512)S(1)} %bitcast.89, bf16[10240]{0:T(1024)(128)(2,1)S(1)} %reduce.5), kind=kOutput, calls=%fused_computation.20.clone.1 | convolution fusion | flops 681574400 | bytes 1505284 | tf_op jit(solution)/shard_map/while/body/eval_jaxpr/fde,fre->fdr/dot_general | solution.py:66
  108.8 0.6 dynamic_slice.23
  110.0 0.1 reduce.5
  110.1 3.4 %fusion.52 = f32[8,1,64,512]{3,2,1,0:T(8,128)S(1)} fusion(f32[8,1,64,512]{3,2,1,0:T(8,128)S(1)} %get-tuple-element.291, s32[]{:T(128)S(6)} %copy.36, bf16[1,64,10240]{2,1,0:T(8,128)(2,1)S(1)} %get-tuple-element.304, s32[10240]{0:T(1024)S(1)} %bitcast.91, s32[512]{0:T(512)S(1)} %bitcast.89, bf16[10240]{0:T(1024)(128)(2,1)S(1)} %reduce.5), kind=kOutput, calls=%fused_computation.20.clone.1 | convolution fusion | flops 681574400 | bytes 1505284 | tf_op jit(solution)/shard_map/while/body/eval_jaxpr/fde,fre->fdr/dot_general | solution.py:66
  113.6 0.6 dynamic_slice.23
  114.8 0.1 reduce.5
  115.0 3.4 %fusion.52 = f32[8,1,64,512]{3,2,1,0:T(8,128)S(1)} fusion(f32[8,1,64,512]{3,2,1,0:T(8,128)S(1)} %get-tuple-element.291, s32[]{:T(128)S(6)} %copy.36, bf16[1,64,10240]{2,1,0:T(8,128)(2,1)S(1)} %get-tuple-element.304, s32[10240]{0:T(1024)S(1)} %bitcast.91, s32[512]{0:T(512)S(1)} %bitcast.89, bf16[10240]{0:T(1024)(128)(2,1)S(1)} %reduce.5), kind=kOutput, calls=%fused_computation.20.clone.1 | convolution fusion | flops 681574400 | bytes 1505284 | tf_op jit(solution)/shard_map/while/body/eval_jaxpr/fde,fre->fdr/dot_general | solution.py:66
  118.4 0.6 dynamic_slice.23
  119.7 0.1 reduce.5
  119.8 3.4 %fusion.52 = f32[8,1,64,512]{3,2,1,0:T(8,128)S(1)} fusion(f32[8,1,64,512]{3,2,1,0:T(8,128)S(1)} %get-tuple-element.291, s32[]{:T(128)S(6)} %copy.36, bf16[1,64,10240]{2,1,0:T(8,128)(2,1)S(1)} %get-tuple-element.304, s32[10240]{0:T(1024)S(1)} %bitcast.91, s32[512]{0:T(512)S(1)} %bitcast.89, bf16[10240]{0:T(1024)(128)(2,1)S(1)} %reduce.5), kind=kOutput, calls=%fused_computation.20.clone.1 | convolution fusion | flops 681574400 | bytes 1505284 | tf_op jit(solution)/shard_map/while/body/eval_jaxpr/fde,fre->fdr/dot_general | solution.py:66
  123.2 0.6 dynamic_slice.23
  124.5 0.1 reduce.5
  124.6 3.4 %fusion.52 = f32[8,1,64,512]{3,2,1,0:T(8,128)S(1)} fusion(f32[8,1,64,512]{3,2,1,0:T(8,128)S(1)} %get-tuple-element.291, s32[]{:T(128)S(6)} %copy.36, bf16[1,64,10240]{2,1,0:T(8,128)(2,1)S(1)} %get-tuple-element.304, s32[10240]{0:T(1024)S(1)} %bitcast.91, s32[512]{0:T(512)S(1)} %bitcast.89, bf16[10240]{0:T(1024)(128)(2,1)S(1)} %reduce.5), kind=kOutput, calls=%fused_computation.20.clone.1 | convolution fusion | flops 681574400 | bytes 1505284 | tf_op jit(solution)/shard_map/while/body/eval_jaxpr/fde,fre->fdr/dot_general | solution.py:66
  128.0 0.6 dynamic_slice.23
  129.3 0.1 reduce.5
  129.4 3.4 %fusion.52 = f32[8,1,64,512]{3,2,1,0:T(8,128)S(1)} fusion(f32[8,1,64,512]{3,2,1,0:T(8,128)S(1)} %get-tuple-element.291, s32[]{:T(128)S(6)} %copy.36, bf16[1,64,10240]{2,1,0:T(8,128)(2,1)S(1)} %get-tuple-element.304, s32[10240]{0:T(1024)S(1)} %bitcast.91, s32[512]{0:T(512)S(1)} %bitcast.89, bf16[10240]{0:T(1024)(128)(2,1)S(1)} %reduce.5), kind=kOutput, calls=%fused_computation.20.clone.1 | convolution fusion | flops 681574400 | bytes 1505284 | tf_op jit(solution)/shard_map/while/body/eval_jaxpr/fde,fre->fdr/dot_general | solution.py:66
  132.8 0.0 copy-start.3
  132.8 0.2 multiply_reduce_fusion
  133.0 0.1 copy.17
  133.1 10.1 %psum.7 = f32[1,4096]{1,0:T(1,128)S(1)} all-reduce(f32[1,4096]{1,0:T(1,128)S(1)} %bitcast.87), channel_id=1, replica_groups=mesh['rows'=8,'dims'=4] {'dims'}, use_global_device_ids=true, to_apply=%region_6.7 | all-reduce | flops 4096 | bytes 32768 | tf_op jit(solution)/shard_map/psum | solution.py:71
  143.2 0.6 fusion.45
  143.9 0.9 subtract_convert_fusion
  (34 shorter events, 0.3 us)
Async XLA Ops:
  7.2 137.7 %reduce-scatter.2.cloned.1.call-start = ((), (), s32[]{:S(2)}) async-start(), calls=%async_computation.1 | async-start | bytes 294912 | tf_op jit(solution)/shard_map/reduce_scatter | solution.py:49
  56.6 0.8 copy-start.1
  56.6 0.8 copy-start.4
  56.7 0.8 copy-start.5
  57.5 5.4 %copy-start.2 = (bf16[1,64,128]{2,1,0:T(8,128)(2,1)S(1)}, bf16[1,64,128]{2,1,0:T(8,128)(2,1)}, u32[]{:S(2)}) copy-start(bf16[1,64,128]{2,1,0:T(8,128)(2,1)} %param.13) | copy-start | bytes 49156
  132.8 10.4 %copy-start.3 = (f32[1,4096]{1,0:T(1,128)S(1)}, f32[1,4096]{1,0:T(1,128)}, u32[]{:S(2)}) copy-start(f32[1,4096]{1,0:T(1,128)} %param.12) | copy-start | bytes 49156
  132.8 11.1 %copy-start = (bf16[1,64,4096]{2,1,0:T(8,128)(2,1)S(1)}, bf16[1,64,4096]{2,1,0:T(8,128)(2,1)}, u32[]{:S(2)}) copy-start(bf16[1,64,4096]{2,1,0:T(8,128)(2,1)} %get-tuple-element.309) | copy-start | bytes 1572868
Sparse Core Ops, SparseCore 0:
  62.8 64.8 reduce-scatter.1
where the time goes:
time: 152 us
  matrix products  73.9 us (49%)
  blocking collectives  38.2 us (25%)
  between operations  14.2 us (9%)
  local copies, waits for them, and re-layouts  11.3 us (7%)
  loops' own time  11 us (7%)
  other arithmetic  3.03 us (2%)
    dot_general x8, matrix products, lookup_block(): jnp.einsum('fdr,fre->fde', table_part, selector, preferred_element_type=j...  38.3 us
    all_gather x1, blocking collectives, shards(): all_grads = lax.all_gather(grad_pooled, 'rows', axis=2, tiled=True)  28.1 us
    dot_general x8, matrix products, gradient_block(): jnp.einsum('fde,fre->fdr', entry_flat, weighted, preferred_element_type=j...  27.4 us
    psum x1, blocking collectives, shards(): norm_total = lax.psum(squares, 'dims')  10.1 us
    dynamic_slice x16, local copies, waits for them, and re-layouts, shards(): lax.scan(lookup_block, jnp.zeros((feat_count, dim_local, entry_count), jn...  9.38 us
    another operation x1, loops' own time, shards(): lax.scan(lookup_block, jnp.zeros((feat_count, dim_local, entry_count), jn...  5.55 us
    another operation x1, loops' own time, shards(): lax.map(gradient_block, jnp.arange(block_count, dtype=jnp.int32))  5.46 us
    dot_general x1, matrix products, shards(): jnp.einsum('fdnk,fnkj->nfdj', picked, onehot, preferred_element_type=jnp....  5.15 us
  transfers between devices with their start and end apart: 1, of which 0 were waited for; matrix products, arithmetic and copies ran while one was open for 25% of the time, Pallas kernels for 0%

commit v1 on v0

--- a/solution.py
+++ b/solution.py
@@ -68,7 +68,11 @@
     grad_blocks = lax.map(gradient_block, jnp.arange(block_count, dtype=jnp.int32))
     row_grad = jnp.moveaxis(grad_blocks, 0, 2).reshape(feat_count, dim_local, row_local)
     squares = jnp.sum(row_grad * row_grad, axis=1)
-    norm_total = lax.psum(squares, "dims")
+    norm_total = squares
+    for hop in (1, 2):
+        norm_total = norm_total + lax.ppermute(
+            norm_total, "dims", [(dev, dev ^ hop) for dev in range(4)]
+        )
     new_accum = accum + norm_total / D
     new_table = (
         table.astype(jnp.float32) - step_size * row_grad / jnp.sqrt(new_accum)[:, None, :]

time: 152 us -> 223 us (1.47)
  waiting for transfers between devices: 0.02 us -> 58.9 us
  matrix products: 73.9 us -> 91.5 us
  blocking collectives: 38.2 us -> 28.2 us
    reduce_scatter x1, waiting for transfers between devices: 0.01 us -> 58.9 us  [shards(): lax.psum_scatter(jnp.einsum('fdnk,fnkj->nfdj', picked, onehot, preferred_...]
    dot_general x8, matrix products: 38.3 us -> 55.1 us  [lookup_block(): jnp.einsum('fdr,fre->fde', table_part, selector, preferred_element_type=j...]
    psum x1 -> x0, blocking collectives: 10.1 us -> none  [shards(): norm_total = lax.psum(squares, 'dims')]
  transfers between devices with their start and end apart: 1 -> 3, of which waited for: 0 -> 1; matrix products, arithmetic and copies ran while one was open for 25% -> 31% of each run, Pallas kernels for 0% -> 0%
where the time goes in v1:
time: 223 us; the launch traced here: 222 us
  matrix products  91.5 us (41%)
  waiting for transfers between devices  58.9 us (26%)
  blocking collectives  28.2 us (13%)
  between operations  14.2 us (6%)
  local copies, waits for them, and re-layouts  12.3 us (6%)
  loops' own time  10.8 us (5%)
  other arithmetic  4.81 us (2%)
    reduce_scatter x1, waiting for transfers between devices, shards(): lax.psum_scatter(jnp.einsum('fdnk,fnkj->nfdj', picked, onehot, preferred_...  58.9 us
    dot_general x8, matrix products, lookup_block(): jnp.einsum('fdr,fre->fde', table_part, selector, preferred_element_type=j...  55.1 us
    all_gather x1, blocking collectives, shards(): all_grads = lax.all_gather(grad_pooled, 'rows', axis=2, tiled=True)  28.2 us
    dot_general x8, matrix products, gradient_block(): jnp.einsum('fde,fre->fdr', entry_flat, weighted, preferred_element_type=j...  27.3 us
    dynamic_slice x16, local copies, waits for them, and re-layouts, shards(): lax.scan(lookup_block, jnp.zeros((feat_count, dim_local, entry_count), jn...  9.35 us
    another operation x1, loops' own time, shards(): lax.map(gradient_block, jnp.arange(block_count, dtype=jnp.int32))  5.46 us
    another operation x1, loops' own time, shards(): lax.scan(lookup_block, jnp.zeros((feat_count, dim_local, entry_count), jn...  5.39 us
    dot_general x1, matrix products, shards(): jnp.einsum('fdnk,fnkj->nfdj', picked, onehot, preferred_element_type=jnp....  5.15 us
  transfers between devices with their start and end apart: 3, of which 1 were waited for; matrix products, arithmetic and copies ran while one was open for 31% of the time, Pallas kernels for 0%

profile of v1, /device:TPU:0, one launch (start us, length us, event | category | flops | bytes accessed | tf_op | source)
XLA Modules:
  0.0 222.4 jit_solution(11633399811877562371)
XLA Ops:
  7.2 0.0 reduce-scatter.2.cloned.1.call-start
  7.2 0.8 reshape_reshape.3
  8.0 0.8 reshape.272
  8.9 0.7 lt.56
  9.7 28.2 %all_gather.3 = bf16[1,64,1024]{2,1,0:T(8,128)(2,1)S(1)} all-gather(bf16[1,64,128]{2,1,0:T(8,128)(2,1)} %param.13), channel_id=1, replica_groups=mesh['rows'=8,'dims'=4] {'rows'}, dimensions={2}, use_global_device_ids=true | all-gather | bytes 147456 | tf_op jit(solution)/shard_map/all_gather | solution.py:55
  37.9 3.9 %fusion.32 = bf16[1,8,8,8,1280]{4,3,2,1,0:T(8,128)(2,1)S(1)} fusion(s32[8,1280]{1,0:T(8,128)} %bitcast.95, bf16[64,8,128]{2,1,0:T(8,128)(2,1)S(1)} %bitcast.84), kind=kOutput, calls=%fused_computation.27 | convolution fusion | flops 169738240 | bytes 1482752 | tf_op jit(solution)/shard_map/fdnj,fnkj->fdnk/dot_general | solution.py:58
  41.8 0.1 copy.16
  41.9 0.1 fusion.43
  42.0 0.0 copy-start
  42.0 38.4 %while.24 = (s32[]{:T(128)}, f32[8,1,64,512]{3,2,1,0:T(8,128)S(1)}, s32[1,1,10240]{2,1,0:T(1,128)S(1)}, s32[8]{0:T(128)S(1)}, bf16[1,1,10240]{2,1,0:T(2,128)(2,1...) while((s32[]{:T(128)}, f32[8,1,64,512]{3,2,1,0:T(8,128)S(1)}, ...), condition=%wide.region_4.5_spmd.clone, body=%wide.region_3.4_spmd.clone.sunk | while | flops 681574912 | bytes 1548423 | solution.py:68
  42.0 0.6 dynamic_slice.23
  43.3 0.1 reduce.5
  43.4 3.4 %fusion.52 = f32[8,1,64,512]{3,2,1,0:T(8,128)S(1)} fusion(f32[8,1,64,512]{3,2,1,0:T(8,128)S(1)} %get-tuple-element.291, s32[]{:T(128)S(6)} %copy.36, bf16[1,64,10240]{2,1,0:T(8,128)(2,1)S(1)} %get-tuple-element.304, s32[10240]{0:T(1024)S(1)} %bitcast.91, s32[512]{0:T(512)S(1)} %bitcast.90, bf16[10240]{0:T(1024)(128)(2,1)S(1)} %reduce.5), kind=kOutput, calls=%fused_computation.20.clone.1 | convolution fusion | flops 681574400 | bytes 1505284 | tf_op jit(solution)/shard_map/while/body/eval_jaxpr/fde,fre->fdr/dot_general | solution.py:66
  46.8 0.6 dynamic_slice.23
  48.1 0.1 reduce.5
  48.2 3.4 %fusion.52 = f32[8,1,64,512]{3,2,1,0:T(8,128)S(1)} fusion(f32[8,1,64,512]{3,2,1,0:T(8,128)S(1)} %get-tuple-element.291, s32[]{:T(128)S(6)} %copy.36, bf16[1,64,10240]{2,1,0:T(8,128)(2,1)S(1)} %get-tuple-element.304, s32[10240]{0:T(1024)S(1)} %bitcast.91, s32[512]{0:T(512)S(1)} %bitcast.90, bf16[10240]{0:T(1024)(128)(2,1)S(1)} %reduce.5), kind=kOutput, calls=%fused_computation.20.clone.1 | convolution fusion | flops 681574400 | bytes 1505284 | tf_op jit(solution)/shard_map/while/body/eval_jaxpr/fde,fre->fdr/dot_general | solution.py:66
  51.6 0.6 dynamic_slice.23
  52.9 0.1 reduce.5
  53.0 3.4 %fusion.52 = f32[8,1,64,512]{3,2,1,0:T(8,128)S(1)} fusion(f32[8,1,64,512]{3,2,1,0:T(8,128)S(1)} %get-tuple-element.291, s32[]{:T(128)S(6)} %copy.36, bf16[1,64,10240]{2,1,0:T(8,128)(2,1)S(1)} %get-tuple-element.304, s32[10240]{0:T(1024)S(1)} %bitcast.91, s32[512]{0:T(512)S(1)} %bitcast.90, bf16[10240]{0:T(1024)(128)(2,1)S(1)} %reduce.5), kind=kOutput, calls=%fused_computation.20.clone.1 | convolution fusion | flops 681574400 | bytes 1505284 | tf_op jit(solution)/shard_map/while/body/eval_jaxpr/fde,fre->fdr/dot_general | solution.py:66
  56.4 0.6 dynamic_slice.23
  57.7 0.1 reduce.5
  57.8 3.4 %fusion.52 = f32[8,1,64,512]{3,2,1,0:T(8,128)S(1)} fusion(f32[8,1,64,512]{3,2,1,0:T(8,128)S(1)} %get-tuple-element.291, s32[]{:T(128)S(6)} %copy.36, bf16[1,64,10240]{2,1,0:T(8,128)(2,1)S(1)} %get-tuple-element.304, s32[10240]{0:T(1024)S(1)} %bitcast.91, s32[512]{0:T(512)S(1)} %bitcast.90, bf16[10240]{0:T(1024)(128)(2,1)S(1)} %reduce.5), kind=kOutput, calls=%fused_computation.20.clone.1 | convolution fusion | flops 681574400 | bytes 1505284 | tf_op jit(solution)/shard_map/while/body/eval_jaxpr/fde,fre->fdr/dot_general | solution.py:66
  61.2 0.6 dynamic_slice.23
  62.5 0.1 reduce.5
  62.6 3.4 %fusion.52 = f32[8,1,64,512]{3,2,1,0:T(8,128)S(1)} fusion(f32[8,1,64,512]{3,2,1,0:T(8,128)S(1)} %get-tuple-element.291, s32[]{:T(128)S(6)} %copy.36, bf16[1,64,10240]{2,1,0:T(8,128)(2,1)S(1)} %get-tuple-element.304, s32[10240]{0:T(1024)S(1)} %bitcast.91, s32[512]{0:T(512)S(1)} %bitcast.90, bf16[10240]{0:T(1024)(128)(2,1)S(1)} %reduce.5), kind=kOutput, calls=%fused_computation.20.clone.1 | convolution fusion | flops 681574400 | bytes 1505284 | tf_op jit(solution)/shard_map/while/body/eval_jaxpr/fde,fre->fdr/dot_general | solution.py:66
  66.0 0.6 dynamic_slice.23
  67.3 0.1 reduce.5
  67.4 3.4 %fusion.52 = f32[8,1,64,512]{3,2,1,0:T(8,128)S(1)} fusion(f32[8,1,64,512]{3,2,1,0:T(8,128)S(1)} %get-tuple-element.291, s32[]{:T(128)S(6)} %copy.36, bf16[1,64,10240]{2,1,0:T(8,128)(2,1)S(1)} %get-tuple-element.304, s32[10240]{0:T(1024)S(1)} %bitcast.91, s32[512]{0:T(512)S(1)} %bitcast.90, bf16[10240]{0:T(1024)(128)(2,1)S(1)} %reduce.5), kind=kOutput, calls=%fused_computation.20.clone.1 | convolution fusion | flops 681574400 | bytes 1505284 | tf_op jit(solution)/shard_map/while/body/eval_jaxpr/fde,fre->fdr/dot_general | solution.py:66
  70.8 0.6 dynamic_slice.23
  72.1 0.1 reduce.5
  72.2 3.4 %fusion.52 = f32[8,1,64,512]{3,2,1,0:T(8,128)S(1)} fusion(f32[8,1,64,512]{3,2,1,0:T(8,128)S(1)} %get-tuple-element.291, s32[]{:T(128)S(6)} %copy.36, bf16[1,64,10240]{2,1,0:T(8,128)(2,1)S(1)} %get-tuple-element.304, s32[10240]{0:T(1024)S(1)} %bitcast.91, s32[512]{0:T(512)S(1)} %bitcast.90, bf16[10240]{0:T(1024)(128)(2,1)S(1)} %reduce.5), kind=kOutput, calls=%fused_computation.20.clone.1 | convolution fusion | flops 681574400 | bytes 1505284 | tf_op jit(solution)/shard_map/while/body/eval_jaxpr/fde,fre->fdr/dot_general | solution.py:66
  75.6 0.6 dynamic_slice.23
  76.9 0.1 reduce.5
  77.0 3.4 %fusion.52 = f32[8,1,64,512]{3,2,1,0:T(8,128)S(1)} fusion(f32[8,1,64,512]{3,2,1,0:T(8,128)S(1)} %get-tuple-element.291, s32[]{:T(128)S(6)} %copy.36, bf16[1,64,10240]{2,1,0:T(8,128)(2,1)S(1)} %get-tuple-element.304, s32[10240]{0:T(1024)S(1)} %bitcast.91, s32[512]{0:T(512)S(1)} %bitcast.90, bf16[10240]{0:T(1024)(128)(2,1)S(1)} %reduce.5), kind=kOutput, calls=%fused_computation.20.clone.1 | convolution fusion | flops 681574400 | bytes 1505284 | tf_op jit(solution)/shard_map/while/body/eval_jaxpr/fde,fre->fdr/dot_general | solution.py:66
  80.4 0.2 multiply_reduce_fusion
  80.6 0.1 collective-permute-start
  80.7 0.0 copy-start.1
  80.8 65.2 %while.25 = (s32[]{:T(128)}, f32[1,64,10240]{2,1,0:T(8,128)}, s32[8]{0:T(128)S(1)}, bf16[1,64,4096]{2,1,0:T(8,128)(2,1)S(1)}, s32[1,1,10240]{2,1,0:T(1,128)S(1)}...) while((s32[]{:T(128)}, f32[1,64,10240]{2,1,0:T(8,128)}, s32[8]{0:T(128)S(1)}, ...), condition=%wide.region_1.2_spmd.clone, body=%wide.region_0.1_spmd.clone.sunk | while | flops 677642752 | bytes 5353649 | solution.py:39
  80.8 0.6 dynamic_slice.25
  82.0 5.4 %fusion.55 = f32[1,64,10240]{2,1,0:T(8,128)} fusion(s32[10240]{0:T(1024)S(1)} %bitcast.92, s32[512]{0:T(512)S(1)} %bitcast.89, f32[1,64,10240]{2,1,0:T(8,128)} %get-tuple-element.264, pred[]{:T(512)S(6)} %compare.3, bf16[1,64,4096]{2,1,0:T(8,128)(2,1)S(1)} %get-tuple-element.275, s32[]{:T(128)S(6)} %select_n.63), kind=kOutput, calls=%fused_computation.5.clone.1 | convolution fusion | flops 677642240 | bytes 5351429 | tf_op jit(solution)/shard_map/while/body/eval_jaxpr/fdr,fre->fde/dot_general | solution.py:35
  87.4 0.6 dynamic_slice.25
  88.7 7.1 %fusion.55 = f32[1,64,10240]{2,1,0:T(8,128)} fusion(s32[10240]{0:T(1024)S(1)} %bitcast.92, s32[512]{0:T(512)S(1)} %bitcast.89, f32[1,64,10240]{2,1,0:T(8,128)} %get-tuple-element.264, pred[]{:T(512)S(6)} %compare.3, bf16[1,64,4096]{2,1,0:T(8,128)(2,1)S(1)} %get-tuple-element.275, s32[]{:T(128)S(6)} %select_n.63), kind=kOutput, calls=%fused_computation.5.clone.1 | convolution fusion | flops 677642240 | bytes 5351429 | tf_op jit(solution)/shard_map/while/body/eval_jaxpr/fdr,fre->fde/dot_general | solution.py:35
  95.8 0.6 dynamic_slice.25
  97.0 7.1 %fusion.55 = f32[1,64,10240]{2,1,0:T(8,128)} fusion(s32[10240]{0:T(1024)S(1)} %bitcast.92, s32[512]{0:T(512)S(1)} %bitcast.89, f32[1,64,10240]{2,1,0:T(8,128)} %get-tuple-element.264, pred[]{:T(512)S(6)} %compare.3, bf16[1,64,4096]{2,1,0:T(8,128)(2,1)S(1)} %get-tuple-element.275, s32[]{:T(128)S(6)} %select_n.63), kind=kOutput, calls=%fused_computation.5.clone.1 | convolution fusion | flops 677642240 | bytes 5351429 | tf_op jit(solution)/shard_map/while/body/eval_jaxpr/fdr,fre->fde/dot_general | solution.py:35
  104.1 0.6 dynamic_slice.25
  105.4 7.1 %fusion.55 = f32[1,64,10240]{2,1,0:T(8,128)} fusion(s32[10240]{0:T(1024)S(1)} %bitcast.92, s32[512]{0:T(512)S(1)} %bitcast.89, f32[1,64,10240]{2,1,0:T(8,128)} %get-tuple-element.264, pred[]{:T(512)S(6)} %compare.3, bf16[1,64,4096]{2,1,0:T(8,128)(2,1)S(1)} %get-tuple-element.275, s32[]{:T(128)S(6)} %select_n.63), kind=kOutput, calls=%fused_computation.5.clone.1 | convolution fusion | flops 677642240 | bytes 5351429 | tf_op jit(solution)/shard_map/while/body/eval_jaxpr/fdr,fre->fde/dot_general | solution.py:35
  112.5 0.6 dynamic_slice.25
  113.8 7.1 %fusion.55 = f32[1,64,10240]{2,1,0:T(8,128)} fusion(s32[10240]{0:T(1024)S(1)} %bitcast.92, s32[512]{0:T(512)S(1)} %bitcast.89, f32[1,64,10240]{2,1,0:T(8,128)} %get-tuple-element.264, pred[]{:T(512)S(6)} %compare.3, bf16[1,64,4096]{2,1,0:T(8,128)(2,1)S(1)} %get-tuple-element.275, s32[]{:T(128)S(6)} %select_n.63), kind=kOutput, calls=%fused_computation.5.clone.1 | convolution fusion | flops 677642240 | bytes 5351429 | tf_op jit(solution)/shard_map/while/body/eval_jaxpr/fdr,fre->fde/dot_general | solution.py:35
  120.9 0.6 dynamic_slice.25
  122.1 7.1 %fusion.55 = f32[1,64,10240]{2,1,0:T(8,128)} fusion(s32[10240]{0:T(1024)S(1)} %bitcast.92, s32[512]{0:T(512)S(1)} %bitcast.89, f32[1,64,10240]{2,1,0:T(8,128)} %get-tuple-element.264, pred[]{:T(512)S(6)} %compare.3, bf16[1,64,4096]{2,1,0:T(8,128)(2,1)S(1)} %get-tuple-element.275, s32[]{:T(128)S(6)} %select_n.63), kind=kOutput, calls=%fused_computation.5.clone.1 | convolution fusion | flops 677642240 | bytes 5351429 | tf_op jit(solution)/shard_map/while/body/eval_jaxpr/fdr,fre->fde/dot_general | solution.py:35
  129.2 0.6 dynamic_slice.25
  130.5 7.1 %fusion.55 = f32[1,64,10240]{2,1,0:T(8,128)} fusion(s32[10240]{0:T(1024)S(1)} %bitcast.92, s32[512]{0:T(512)S(1)} %bitcast.89, f32[1,64,10240]{2,1,0:T(8,128)} %get-tuple-element.264, pred[]{:T(512)S(6)} %compare.3, bf16[1,64,4096]{2,1,0:T(8,128)(2,1)S(1)} %get-tuple-element.275, s32[]{:T(128)S(6)} %select_n.63), kind=kOutput, calls=%fused_computation.5.clone.1 | convolution fusion | flops 677642240 | bytes 5351429 | tf_op jit(solution)/shard_map/while/body/eval_jaxpr/fdr,fre->fde/dot_general | solution.py:35
  137.6 0.6 dynamic_slice.25
  138.8 7.1 %fusion.55 = f32[1,64,10240]{2,1,0:T(8,128)} fusion(s32[10240]{0:T(1024)S(1)} %bitcast.92, s32[512]{0:T(512)S(1)} %bitcast.89, f32[1,64,10240]{2,1,0:T(8,128)} %get-tuple-element.264, pred[]{:T(512)S(6)} %compare.3, bf16[1,64,4096]{2,1,0:T(8,128)(2,1)S(1)} %get-tuple-element.275, s32[]{:T(128)S(6)} %select_n.63), kind=kOutput, calls=%fused_computation.5.clone.1 | convolution fusion | flops 677642240 | bytes 5351429 | tf_op jit(solution)/shard_map/while/body/eval_jaxpr/fdr,fre->fde/dot_general | solution.py:35
  145.9 0.1 bitcast_select_fusion
  146.0 1.9 convert_element_type.41
  147.9 0.2 copy.18
  148.2 1.6 collective-permute-start.1
  149.7 5.1 %fusion.39 = f32[8,1,64,128]{3,2,0,1:T(8,128)} fusion(s32[8,1280]{1,0:T(8,128)S(1)} %bitcast_select_fusion, s32[8,1280]{1,0:T(8,128)S(1)} %bitcast.96, bf16[64,8,1280]{2,1,0:T(8,128)(2,1)S(1)} %bitcast.82), kind=kOutput, calls=%fused_computation.34 | convolution fusion | flops 171704320 | bytes 1654784 | tf_op jit(solution)/shard_map/fdnk,fnkj->nfdj/dot_general | solution.py:50
  154.9 0.0 reduce-scatter.2.cloned.1.call-update
  154.9 0.1 copy.17
  155.0 0.6 fusion.45
  155.7 0.9 subtract_convert_fusion
  156.6 58.9 %reduce-scatter.2.cloned.1.call-done = f32[1,1,64,128]{3,2,0,1:T(8,128)} async-done(((f32[8,1,64,128]{3,2,0,1:T(8,128)}), f32[1,1,64,128]{3,2,0,1:T(8,128)}) %reduce-scatter.2.cloned.1.call-update) | async-done | bytes 32784 | tf_op jit(solution)/shard_map/reduce_scatter | solution.py:49
  (36 shorter events, 0.3 us)
Async XLA Ops:
  7.2 208.4 %reduce-scatter.2.cloned.1.call-start = ((), (), s32[]{:S(2)}) async-start(), calls=%async_computation.1 | async-start | bytes 294912 | tf_op jit(solution)/shard_map/reduce_scatter | solution.py:49
  42.0 38.8 %copy-start = (bf16[1,64,4096]{2,1,0:T(8,128)(2,1)S(1)}, bf16[1,64,4096]{2,1,0:T(8,128)(2,1)}, u32[]{:S(2)}) copy-start(bf16[1,64,4096]{2,1,0:T(8,128)(2,1)} %param.11) | copy-start | bytes 1572868
  80.6 67.5 %collective-permute-start = (f32[1,4096]{1,0:T(1,128)S(1)}, f32[1,4096]{1,0:T(1,128)S(1)}, u32[]{:S(2)}, u32[]{:S(2)}) collective-permute-start(f32[1,4096]{1,0:T(1,128)S(1)} %bitcast.87), channel_id=1, source_target_pairs={{0,1},{1,0},{2,3},{3,2},{4,5},{5,4},{6,7},{7,6},{8,9},{9,8},{10,11... | collective-permute-start | bytes 49160 | tf_op jit(solution)/shard_map/ppermute | solution.py:73
  80.7 65.2 %copy-start.1 = (s32[1,1,8,1280]{3,2,1,0:T(8,128)S(1)}, s32[1,1,8,1280]{3,2,1,0:T(8,128)}, u32[]{:S(2)}) copy-start(s32[1,1,8,1280]{3,2,1,0:T(8,128)} %param.16) | copy-start | bytes 122884
  80.8 65.2 %copy-start.3 = (s32[1,1,8]{2,1,0:T(1,128)S(1)}, s32[1,1,8]{2,1,0:T(1,128)}, u32[]{:S(2)}) copy-start(s32[1,1,8]{2,1,0:T(1,128)} %param.17) | copy-start | bytes 100
  146.0 3.7 %copy-start.4 = (s32[1,1,8,1280]{3,2,1,0:T(8,128)S(1)}, s32[1,1,8,1280]{3,2,1,0:T(8,128)}, u32[]{:S(2)}) copy-start(s32[1,1,8,1280]{3,2,1,0:T(8,128)} %param.14) | copy-start | bytes 122884
  148.2 6.8 %collective-permute-start.1 = (f32[1,4096]{1,0:T(1,128)S(1)}, f32[1,4096]{1,0:T(1,128)S(1)}, u32[]{:S(2)}, u32[]{:S(2)}) collective-permute-start(f32[1,4096]{1,0:T(1,128)S(1)} %add.57), channel_id=1, source_target_pairs={{0,2},{1,3},{2,0},{3,1},{4,6},{5,7},{6,4},{7,5},{8,10},{9,11},{10,... | collective-permute-start | bytes 49160 | tf_op jit(solution)/shard_map/ppermute | solution.py:73
  149.7 5.3 %copy-start.2 = (f32[1,4096]{1,0:T(1,128)S(1)}, f32[1,4096]{1,0:T(1,128)}, u32[]{:S(2)}) copy-start(f32[1,4096]{1,0:T(1,128)} %param.12) | copy-start | bytes 49156
Sparse Core Ops, SparseCore 0:
  155.0 60.4 reduce-scatter.1
